TPU v7x, 256 devices: a whole 4x4x8 slice. The times are simulated.
256 devices in a mesh: row: 16 (over y, x), col: 16 (over z, core).
Axes of the slice: x: 4, y: 4, z: 8, core: 2. Of those that a mesh axis runs over, the one named last changes fastest.
Arguments:
- rhs: float32 [128, 32768], P('row', 'col'), may hold values from -60 to 60
- flex_tiles: float32 [131072, 2048], P('row', 'col'), may hold values from -0.25 to 0.25
- flex_cols: int32 [256, 64], P('row', 'col'), may hold values from 0 to 15, as said below
- stiff_tiles: float32 [131072, 2048], P('row', 'col'), may hold values from -0.25 to 0.25
- stiff_cols: int32 [256, 64], P('row', 'col'), may hold values from 0 to 15, as said below
- deflation: float32 [512, 32768], P('row', 'col'), may hold values from -0.375 to 0.375
- coarse_rows: float32 [8192, 8192], P(('row', 'col')), may hold values from -5 to 5, as said below
- face_rows: int32 [64, 2048], P('row', 'col'), may hold values from 0 to 2047, as said below
- face_len: int32 [16, 64], P('row', 'col'), may hold values from 0 to 128, as said below
Outputs:
- solution: float32 [128, 32768], P('row', 'col')
- residual: float32 [128, 32768], P('row', 'col')
- correction: float32 [128, 32768], P('row', 'col')
Inputs may be any that keep to these rules, and one draw needn't show every extreme that they name: `flex_cols`: row b of a subdomain's block list names 4 different block columns, the first being b. `stiff_cols`: row b of a subdomain's block list names 4 different block columns, the first being b. `coarse_rows`: the whole matrix is symmetric. `face_rows`: the four lists of a subdomain name 512 different multipliers of it. `face_len`: the two subdomains of a face give it the same length; faces on the grid's boundary have length 0, inner faces at least 32.
All inputs are finite; a program needn't handle non-finite values.
Results may differ from a plain program's by a relative error of at most 0.0003.
Values sent between devices are 32-bit elements; how exact they have to be, the bound alone decides.
A program may use at most 64 MiB of HBM per device.

v0:
```python
import jax
import jax.numpy as jnp
from jax import lax
from jax.sharding import PartitionSpec as P

ITERS = 3
PRECISE = lax.Precision.HIGHEST


def with_halo(cells, sides, width):
    for axis, dim in sides:
        count = lax.axis_size(axis)
        ends = count - 1
        head = lax.slice_in_dim(cells, 0, width, axis=dim)
        tail = lax.slice_in_dim(cells, cells.shape[dim] - width, cells.shape[dim], axis=dim)
        cells = jnp.concatenate(
            [
                lax.ppermute(tail, axis, [(i, (i + 1) % count) for i in range(ends)]),
                cells,
                lax.ppermute(head, axis, [((i + 1) % count, i) for i in range(ends)]),
            ],
            axis=dim,
        )
    return cells


def sparse_forward(vector, tile_set, columns):
    load_count = vector.shape[0]
    blocks, per_row = columns.shape
    tile_width = tile_set.shape[-1]
    pieces = vector.reshape(load_count, blocks, tile_width)
    picked = jnp.take(pieces, columns.reshape(-1), axis=1).reshape(
        load_count, blocks, per_row, tile_width
    )
    product = jnp.einsum("lbkw,bkwv->lbv", picked, tile_set, precision=PRECISE)
    return product.reshape(load_count, blocks * tile_width)


def sparse_backward(vector, tile_set, columns):
    load_count = vector.shape[0]
    blocks, per_row = columns.shape
    tile_width = tile_set.shape[-1]
    pieces = vector.reshape(load_count, blocks, tile_width)
    product = jnp.einsum("lbv,bkwv->lbkw", pieces, tile_set, precision=PRECISE)
    onehot = (columns[:, :, None] == jnp.arange(blocks, dtype=jnp.int32)[None, None, :]).astype(
        jnp.float32
    )
    summed = jnp.einsum("lbkw,bkj->ljw", product, onehot, precision=PRECISE)
    return summed.reshape(load_count, blocks * tile_width)


def pair_totals(first_field, second_field, third_field, fourth_field):
    return lax.psum(
        (jnp.sum(first_field * second_field, axis=1), jnp.sum(third_field * fourth_field, axis=1)),
        ("row", "col"),
    )


def shards(
    rhs, flex_tiles, flex_cols, stiff_tiles, stiff_cols, deflation, coarse_rows, face_rows, face_len
):
    blocks, per_row = flex_cols.shape
    tile_width = flex_tiles.shape[1]
    flex_set = flex_tiles.reshape(blocks, per_row, tile_width, tile_width)
    stiff_set = stiff_tiles.reshape(blocks, per_row, tile_width, tile_width)
    face_width = face_rows.shape[1]
    flat_index = face_rows.reshape(-1)
    slots = jnp.arange(face_width, dtype=jnp.int32)
    live_mask = (slots[None, :] < face_len.reshape(4, 1)).astype(jnp.float32)

    def face_part(vector):
        load_count = vector.shape[0]
        traces = jnp.take(vector, flat_index, axis=1).reshape(load_count, 4, face_width)
        across_rows = with_halo(traces[:, 0:2], (("row", 1),), 1)
        across_cols = with_halo(traces[:, 2:4], (("col", 1),), 1)
        partner = jnp.stack(
            [across_rows[:, 0], across_rows[:, 3], across_cols[:, 0], across_cols[:, 3]], axis=1
        )
        jump_values = (traces - partner) * live_mask[None]
        return (
            jnp.zeros_like(vector)
            .at[:, flat_index]
            .add(jump_values.reshape(load_count, 4 * face_width))
        )

    def operate(vector):
        coupling = face_part(vector)
        after_flex = sparse_forward(vector, flex_set, flex_cols)
        after_stiff = sparse_forward(after_flex, stiff_set, stiff_cols)
        back_stiff = sparse_backward(after_stiff, stiff_set, stiff_cols)
        local_part = sparse_backward(back_stiff, flex_set, flex_cols)
        return vector + local_part + coupling

    def precondition(vector):
        coefficients = jnp.einsum("lm,dm->ld", vector, deflation, precision=PRECISE)
        energy = jnp.einsum(
            "ln,dn->ld",
            lax.all_gather(coefficients, ("row", "col"), axis=1, tiled=True),
            coarse_rows,
            precision=PRECISE,
        )
        return vector + jnp.einsum("ld,dm->lm", energy, deflation, precision=PRECISE)

    residual = rhs
    solution = jnp.zeros_like(rhs)
    correction = precondition(residual)
    direction = correction
    image = operate(direction)
    curvature_sum, descent_sum = pair_totals(direction, image, residual, direction)
    for iteration in range(ITERS):
        step_size = (descent_sum / curvature_sum)[:, None]
        solution = solution + step_size * direction
        residual = residual - step_size * image
        correction = precondition(residual)
        if iteration + 1 < ITERS:
            cross_sum = lax.psum(jnp.sum(correction * image, axis=1), ("row", "col"))
            blend = -cross_sum / curvature_sum
            direction = correction + blend[:, None] * direction
            image = operate(direction)
            curvature_sum, descent_sum = pair_totals(direction, image, residual, direction)
    return (solution, residual, correction)


def solution(mesh):
    return jax.shard_map(
        shards,
        mesh=mesh,
        in_specs=(
            P("row", "col"),
            P("row", "col"),
            P("row", "col"),
            P("row", "col"),
            P("row", "col"),
            P("row", "col"),
            P(("row", "col"), None),
            P("row", "col"),
            P("row", "col"),
        ),
        out_specs=(P("row", "col"), P("row", "col"), P("row", "col")),
        check_vma=False,
    )
```

profile of v0, /device:TPU:1, one launch (start us, length us, event | category | flops | bytes accessed | tf_op | source)
XLA Modules:
  0.0 747.8 jit_solution(5366016694959184341)
XLA Ops:
  3.4 67.8 %all-gather = f32[256,32,8]{1,2,0:T(8,128)S(1)} all-gather(f32[1,32,8]{1,2,0:T(8,128)S(1)} %convolution_bitcast_fusion.21), channel_id=1, replica_groups=mesh['row'=16,'col'=16] {'row','col'}, dimensions={0}, use_global_device_ids=true | all-gather | bytes 263168 | tf_op jit(solution)/shard_map/all_gather | solution.py:98
  84.8 3.8 convolution_bitcast_fusion.17
  89.4 4.0 convolution_bitcast_fusion.16
  93.5 3.6 convolution_bitcast_fusion.5
  97.4 3.6 convolution_bitcast_fusion.4
  102.2 4.2 scatter_custom_fusion
  106.9 78.0 %all-reduce.2 = (f32[8]{0:T(128)S(1)}, f32[8]{0:T(128)S(1)}) all-reduce(f32[8]{0:T(128)S(1)} %get-tuple-element.10, f32[8]{0:T(128)S(1)} %get-tuple-element.9), channel_id=1, replica_groups=mesh['row'=16,'col'=16] {'row','col'}, use_global_device_ids=true, to_apply=%region_1.2 | all-reduce | flops 16 | bytes 128 | tf_op jit(solution)/shard_map/psum | solution.py:53
  185.2 60.6 %all-gather.1 = f32[256,32,8]{1,2,0:T(8,128)S(1)} all-gather(f32[1,32,8]{1,2,0:T(8,128)S(1)} %convolution_bitcast_fusion.20), channel_id=1, replica_groups=mesh['row'=16,'col'=16] {'row','col'}, dimensions={0}, use_global_device_ids=true | all-gather | bytes 263168 | tf_op jit(solution)/shard_map/all_gather | solution.py:98
  247.8 75.0 %psum.58 = f32[8]{0:T(128)S(1)} all-reduce(f32[8]{0:T(128)S(1)} %get-tuple-element.31), channel_id=1, replica_groups=mesh['row'=16,'col'=16] {'row','col'}, use_global_device_ids=true, to_apply=%region_6.9 | all-reduce | flops 8 | bytes 64 | tf_op jit(solution)/shard_map/psum | solution.py:116
  327.5 4.5 collective-permute-start.6
  335.0 3.8 convolution_bitcast_fusion.15
  339.7 4.0 convolution_bitcast_fusion.14
  347.6 3.6 convolution_bitcast_fusion.2
  352.4 3.9 scatter_custom_fusion.1
  356.8 77.0 %all-reduce.1 = (f32[8]{0:T(128)S(1)}, f32[8]{0:T(128)S(1)}) all-reduce(f32[8]{0:T(128)S(1)} %get-tuple-element.8, f32[8]{0:T(128)S(1)} %get-tuple-element.7), channel_id=1, replica_groups=mesh['row'=16,'col'=16] {'row','col'}, use_global_device_ids=true, to_apply=%region_8.11 | all-reduce | flops 16 | bytes 128 | tf_op jit(solution)/shard_map/psum | solution.py:53
  434.1 61.9 %all-gather.2 = f32[256,32,8]{1,2,0:T(8,128)S(1)} all-gather(f32[1,32,8]{1,2,0:T(8,128)S(1)} %convolution_bitcast_fusion.19), channel_id=1, replica_groups=mesh['row'=16,'col'=16] {'row','col'}, dimensions={0}, use_global_device_ids=true | all-gather | bytes 263168 | tf_op jit(solution)/shard_map/all_gather | solution.py:98
  498.0 73.7 %psum.61 = f32[8]{0:T(128)S(1)} all-reduce(f32[8]{0:T(128)S(1)} %get-tuple-element.33), channel_id=1, replica_groups=mesh['row'=16,'col'=16] {'row','col'}, use_global_device_ids=true, to_apply=%region_13.16 | all-reduce | flops 8 | bytes 64 | tf_op jit(solution)/shard_map/psum | solution.py:116
  573.4 3.8 collective-permute-start.10
  583.8 3.8 convolution_bitcast_fusion.13
  588.4 4.0 convolution_bitcast_fusion.12
  596.4 3.6 convolution_bitcast_fusion
  601.1 3.9 scatter_custom_fusion.2
  605.5 77.2 %all-reduce = (f32[8]{0:T(128)S(1)}, f32[8]{0:T(128)S(1)}) all-reduce(f32[8]{0:T(128)S(1)} %get-tuple-element.6, f32[8]{0:T(128)S(1)} %get-tuple-element.5), channel_id=1, replica_groups=mesh['row'=16,'col'=16] {'row','col'}, use_global_device_ids=true, to_apply=%region_15.18 | all-reduce | flops 16 | bytes 128 | tf_op jit(solution)/shard_map/psum | solution.py:53
  683.7 61.3 %all-gather.3 = f32[256,32,8]{1,2,0:T(8,128)S(1)} all-gather(f32[1,32,8]{1,2,0:T(8,128)S(1)} %convolution_bitcast_fusion.18), channel_id=1, replica_groups=mesh['row'=16,'col'=16] {'row','col'}, dimensions={0}, use_global_device_ids=true | all-gather | bytes 263168 | tf_op jit(solution)/shard_map/all_gather | solution.py:98
  (161 shorter events, 55.3 us)
Async XLA Ops:
  0.6 71.3 %copy-start = (f32[32,8192]{1,0:T(8,128)S(1)}, f32[32,8192]{1,0:T(8,128)}, u32[]{:S(2)}) copy-start(f32[32,8192]{1,0:T(8,128)} %param.19) | copy-start | bytes 3145732
  0.6 72.2 %copy-start.8 = (f32[8,2048]{1,0:T(8,128)S(1)}, f32[8,2048]{1,0:T(8,128)}, u32[]{:S(2)}) copy-start(f32[8,2048]{1,0:T(8,128)} %param.13) | copy-start | bytes 196612
  0.7 72.2 %copy-start.7 = (f32[32,2048]{1,0:T(8,128)S(1)}, f32[32,2048]{1,0:T(8,128)}, u32[]{:S(2)}) copy-start(f32[32,2048]{1,0:T(8,128)} %param.18) | copy-start | bytes 786436
  3.4 80.1 %copy-start.11 = (s32[16,4]{0,1:T(4,128)S(1)}, s32[16,4]{0,1:T(4,128)}, u32[]{:S(2)}) copy-start(s32[16,4]{0,1:T(4,128)} %param.15) | copy-start | bytes 772
  3.4 80.3 %copy-start.10 = (s32[16,4]{0,1:T(4,128)S(1)}, s32[16,4]{0,1:T(4,128)}, u32[]{:S(2)}) copy-start(s32[16,4]{0,1:T(4,128)} %param.17) | copy-start | bytes 772
  3.4 80.5 %copy-start.13 = (s32[1,4]{1,0:T(1,128)S(1)}, s32[1,4]{1,0:T(1,128)}, u32[]{:S(2)}) copy-start(s32[1,4]{1,0:T(1,128)} %param.21) | copy-start | bytes 52
  74.7 27.1 %collective-permute-start = (f32[8,1,128]{2,0,1:T(8,128)S(1)}, f32[8,1,128]{2,0,1:T(8,128)S(1)}, u32[]{:S(2)}, u32[]{:S(2)}) collective-permute-start(f32[8,1,128]{2,0,1:T(8,128)S(1)} %copy.118), channel_id=1, source_target_pairs={{0,16},{16,32},{32,48},{48,64},{64,80},{80,96},{96,112},{112,128},... | collective-permute-start | bytes 12296 | tf_op jit(solution)/shard_map/ppermute | solution.py:18
  77.4 24.4 %collective-permute-start.1 = (f32[8,1,128]{2,0,1:T(8,128)S(1)}, f32[8,1,128]{2,0,1:T(8,128)S(1)}, u32[]{:S(2)}, u32[]{:S(2)}) collective-permute-start(f32[8,1,128]{2,0,1:T(8,128)S(1)} %copy.119), channel_id=1, source_target_pairs={{16,0},{32,16},{48,32},{64,48},{80,64},{96,80},{112,96},{128,112},... | collective-permute-start | bytes 12296 | tf_op jit(solution)/shard_map/ppermute | solution.py:20
  78.8 23.0 %collective-permute-start.2 = (f32[8,1,128]{2,0,1:T(8,128)S(1)}, f32[8,1,128]{2,0,1:T(8,128)S(1)}, u32[]{:S(2)}, u32[]{:S(2)}) collective-permute-start(f32[8,1,128]{2,0,1:T(8,128)S(1)} %copy.120), channel_id=1, source_target_pairs={{0,1},{1,2},{2,3},{3,4},{4,5},{5,6},{6,7},{7,8},{8,9},{9,10},{10,1... | collective-permute-start | bytes 12296 | tf_op jit(solution)/shard_map/ppermute | solution.py:18
  80.8 21.1 %collective-permute-start.3 = (f32[8,1,128]{2,0,1:T(8,128)S(1)}, f32[8,1,128]{2,0,1:T(8,128)S(1)}, u32[]{:S(2)}, u32[]{:S(2)}) collective-permute-start(f32[8,1,128]{2,0,1:T(8,128)S(1)} %copy.121), channel_id=1, source_target_pairs={{1,0},{2,1},{3,2},{4,3},{5,4},{6,5},{7,6},{8,7},{9,8},{10,9},{11,1... | collective-permute-start | bytes 12296 | tf_op jit(solution)/shard_map/ppermute | solution.py:20
  89.3 4.2 copy-start.1
  89.4 8.0 %copy-start.4 = (f32[8192,128]{1,0:T(8,128)S(1)}, f32[8192,128]{1,0:T(8,128)}, u32[]{:S(2)}) copy-start(f32[8192,128]{1,0:T(8,128)} %param.14) | copy-start | bytes 12582916
  93.4 8.0 %copy-start.12 = (s32[4,128]{1,0:T(4,128)S(1)}, s32[4,128]{1,0:T(4,128)}, u32[]{:S(2)}) copy-start(s32[4,128]{1,0:T(4,128)} %param.20) | copy-start | bytes 6148
  324.6 27.4 %collective-permute-start.4 = (f32[8,1,128]{2,0,1:T(8,128)S(1)}, f32[8,1,128]{2,0,1:T(8,128)S(1)}, u32[]{:S(2)}, u32[]{:S(2)}) collective-permute-start(f32[8,1,128]{2,0,1:T(8,128)S(1)} %copy.122), channel_id=1, source_target_pairs={{0,16},{16,32},{32,48},{48,64},{64,80},{80,96},{96,112},{112,128},... | collective-permute-start | bytes 12296 | tf_op jit(solution)/shard_map/ppermute | solution.py:18
  326.2 25.8 %collective-permute-start.5 = (f32[8,1,128]{2,0,1:T(8,128)S(1)}, f32[8,1,128]{2,0,1:T(8,128)S(1)}, u32[]{:S(2)}, u32[]{:S(2)}) collective-permute-start(f32[8,1,128]{2,0,1:T(8,128)S(1)} %copy.123), channel_id=1, source_target_pairs={{16,0},{32,16},{48,32},{64,48},{80,64},{96,80},{112,96},{128,112},... | collective-permute-start | bytes 12296 | tf_op jit(solution)/shard_map/ppermute | solution.py:20
  327.5 24.5 %collective-permute-start.6 = (f32[8,1,128]{2,0,1:T(8,128)S(1)}, f32[8,1,128]{2,0,1:T(8,128)S(1)}, u32[]{:S(2)}, u32[]{:S(2)}) collective-permute-start(f32[8,1,128]{2,0,1:T(8,128)S(1)} %copy.124), channel_id=1, source_target_pairs={{0,1},{1,2},{2,3},{3,4},{4,5},{5,6},{6,7},{7,8},{8,9},{9,10},{10,1... | collective-permute-start | bytes 12296 | tf_op jit(solution)/shard_map/ppermute | solution.py:18
  332.1 19.9 %collective-permute-start.7 = (f32[8,1,128]{2,0,1:T(8,128)S(1)}, f32[8,1,128]{2,0,1:T(8,128)S(1)}, u32[]{:S(2)}, u32[]{:S(2)}) collective-permute-start(f32[8,1,128]{2,0,1:T(8,128)S(1)} %copy.125), channel_id=1, source_target_pairs={{1,0},{2,1},{3,2},{4,3},{5,4},{6,5},{7,6},{8,7},{9,8},{10,9},{11,1... | collective-permute-start | bytes 12296 | tf_op jit(solution)/shard_map/ppermute | solution.py:20
  339.6 8.0 %copy-start.5 = (f32[8192,128]{1,0:T(8,128)S(1)}, f32[8192,128]{1,0:T(8,128)}, u32[]{:S(2)}) copy-start(f32[8192,128]{1,0:T(8,128)} %param.14) | copy-start | bytes 12582916
  573.4 27.4 %collective-permute-start.10 = (f32[8,1,128]{2,0,1:T(8,128)S(1)}, f32[8,1,128]{2,0,1:T(8,128)S(1)}, u32[]{:S(2)}, u32[]{:S(2)}) collective-permute-start(f32[8,1,128]{2,0,1:T(8,128)S(1)} %copy.128), channel_id=1, source_target_pairs={{0,1},{1,2},{2,3},{3,4},{4,5},{5,6},{6,7},{7,8},{8,9},{9,10},{10,1... | collective-permute-start | bytes 12296 | tf_op jit(solution)/shard_map/ppermute | solution.py:18
  577.3 23.5 %collective-permute-start.11 = (f32[8,1,128]{2,0,1:T(8,128)S(1)}, f32[8,1,128]{2,0,1:T(8,128)S(1)}, u32[]{:S(2)}, u32[]{:S(2)}) collective-permute-start(f32[8,1,128]{2,0,1:T(8,128)S(1)} %copy.129), channel_id=1, source_target_pairs={{1,0},{2,1},{3,2},{4,3},{5,4},{6,5},{7,6},{8,7},{9,8},{10,9},{11,1... | collective-permute-start | bytes 12296 | tf_op jit(solution)/shard_map/ppermute | solution.py:20
  579.2 21.5 %collective-permute-start.8 = (f32[8,1,128]{2,0,1:T(8,128)S(1)}, f32[8,1,128]{2,0,1:T(8,128)S(1)}, u32[]{:S(2)}, u32[]{:S(2)}) collective-permute-start(f32[8,1,128]{2,0,1:T(8,128)S(1)} %copy.126), channel_id=1, source_target_pairs={{0,16},{16,32},{32,48},{48,64},{64,80},{80,96},{96,112},{112,128},... | collective-permute-start | bytes 12296 | tf_op jit(solution)/shard_map/ppermute | solution.py:18
  581.3 19.5 %collective-permute-start.9 = (f32[8,1,128]{2,0,1:T(8,128)S(1)}, f32[8,1,128]{2,0,1:T(8,128)S(1)}, u32[]{:S(2)}, u32[]{:S(2)}) collective-permute-start(f32[8,1,128]{2,0,1:T(8,128)S(1)} %copy.127), channel_id=1, source_target_pairs={{16,0},{32,16},{48,32},{64,48},{80,64},{96,80},{112,96},{128,112},... | collective-permute-start | bytes 12296 | tf_op jit(solution)/shard_map/ppermute | solution.py:20
  588.4 8.0 %copy-start.6 = (f32[8192,128]{1,0:T(8,128)S(1)}, f32[8192,128]{1,0:T(8,128)}, u32[]{:S(2)}) copy-start(f32[8192,128]{1,0:T(8,128)} %param.14) | copy-start | bytes 12582916
  683.5 64.1 %copy-start.9 = (f32[8,2048]{1,0:T(8,128)}, f32[8,2048]{1,0:T(8,128)S(1)}, u32[]{:S(2)}) copy-start(f32[8,2048]{1,0:T(8,128)S(1)} %get-tuple-element.29) | copy-start | bytes 196612
  (2 other events, 8.3 us)
where the time goes:
time: 753 us; the launch traced here: 748 us
  blocking collectives  633 us (84%)
  matrix products  54.8 us (7%)
  starting transfers between devices  27.5 us (4%)
  other arithmetic  17 us (2%)
  local copies, waits for them, and re-layouts  14.1 us (2%)
    all_gather x4, blocking collectives, precondition(): lax.all_gather(coefficients, ('row', 'col'), axis=1, tiled=True)  252 us
    psum x3, blocking collectives, pair_totals(): lax.psum((jnp.sum(first_field * second_field, axis=1), jnp.sum(third_fiel...  232 us
    psum x2, blocking collectives, shards(): cross_sum = lax.psum(jnp.sum(correction * image, axis=1), ('row', 'col'))  149 us
    dot_general x6, matrix products, sparse_forward(): product = jnp.einsum('lbkw,bkwv->lbv', picked, tile_set, precision=PRECISE)  23.5 us
    dot_general x6, matrix products, sparse_backward(): product = jnp.einsum('lbv,bkwv->lbkw', pieces, tile_set, precision=PRECISE)  21.4 us
    ppermute x6, starting transfers between devices, with_halo(): lax.ppermute(tail, axis, [(i, (i + 1) % count) for i in range(ends)])  16.4 us
  transfers between devices with their start and end apart: 12, of which 0 were waited for; matrix products, arithmetic and copies ran while one was open for 7% of the time, Pallas kernels for 0%

commit v1 on v0

--- a/solution.py
+++ b/solution.py
@@ -113,7 +113,7 @@
         residual = residual - step_size * image
         correction = precondition(residual)
         if iteration + 1 < ITERS:
-            cross_sum = lax.psum(jnp.sum(correction * image, axis=1), ("row", "col"))
+            cross_sum = lax.psum(lax.psum(jnp.sum(correction * image, axis=1), "col"), "row")
             blend = -cross_sum / curvature_sum
             direction = correction + blend[:, None] * direction
             image = operate(direction)

time: 753 us -> 722 us (0.959)
  blocking collectives: 633 us -> 588 us
  starting transfers between devices: 27.5 us -> 41.7 us
    psum x2 -> x4, blocking collectives: 149 us -> 108 us  [the longest x2 61.8 us: shards(): lax.psum(lax.psum(jnp.sum(correction * image, axis=1), 'col'), 'row')]
    ppermute x6, starting transfers between devices: 16.4 us -> 28.4 us  [with_halo(): lax.ppermute(tail, axis, [(i, (i + 1) % count) for i in range(ends)])]
  transfers between devices with their start and end apart: 12 -> 12, of which waited for: 0 -> 0; matrix products, arithmetic and copies ran while one was open for 7% -> 8% of each run, Pallas kernels for 0% -> 0%
where the time goes in v1:
time: 722 us; the launch traced here: 717 us
  blocking collectives  588 us (81%)
  matrix products  54.8 us (8%)
  starting transfers between devices  41.7 us (6%)
  other arithmetic  16.7 us (2%)
  local copies, waits for them, and re-layouts  14.1 us (2%)
    all_gather x4, blocking collectives, precondition(): lax.all_gather(coefficients, ('row', 'col'), axis=1, tiled=True)  250 us
    psum x3, blocking collectives, pair_totals(): lax.psum((jnp.sum(first_field * second_field, axis=1), jnp.sum(third_fiel...  229 us
    psum x2, blocking collectives, shards(): lax.psum(lax.psum(jnp.sum(correction * image, axis=1), 'col'), 'row')  61.8 us
    psum x2, blocking collectives, shards(): lax.psum(jnp.sum(correction * image, axis=1), 'col')  46.1 us
    ppermute x6, starting transfers between devices, with_halo(): lax.ppermute(tail, axis, [(i, (i + 1) % count) for i in range(ends)])  28.4 us
    dot_general x6, matrix products, sparse_forward(): product = jnp.einsum('lbkw,bkwv->lbv', picked, tile_set, precision=PRECISE)  23.5 us
    dot_general x6, matrix products, sparse_backward(): product = jnp.einsum('lbv,bkwv->lbkw', pieces, tile_set, precision=PRECISE)  21.4 us
  transfers between devices with their start and end apart: 12, of which 0 were waited for; matrix products, arithmetic and copies ran while one was open for 8% of the time, Pallas kernels for 0%

profile of v1, /device:TPU:1, one launch (start us, length us, event | category | flops | bytes accessed | tf_op | source)
XLA Modules:
  0.0 717.0 jit_solution(17573783131997306341)
XLA Ops:
  3.4 67.8 %all-gather = f32[256,32,8]{1,2,0:T(8,128)S(1)} all-gather(f32[1,32,8]{1,2,0:T(8,128)S(1)} %convolution_bitcast_fusion.21), channel_id=1, replica_groups=mesh['row'=16,'col'=16] {'row','col'}, dimensions={0}, use_global_device_ids=true | all-gather | bytes 263168 | tf_op jit(solution)/shard_map/all_gather | solution.py:98
  84.7 3.8 convolution_bitcast_fusion.17
  89.3 4.0 convolution_bitcast_fusion.16
  97.3 3.6 convolution_bitcast_fusion.4
  102.1 3.9 scatter_custom_fusion
  106.5 78.0 %all-reduce.2 = (f32[8]{0:T(128)S(1)}, f32[8]{0:T(128)S(1)}) all-reduce(f32[8]{0:T(128)S(1)} %get-tuple-element.10, f32[8]{0:T(128)S(1)} %get-tuple-element.9), channel_id=1, replica_groups=mesh['row'=16,'col'=16] {'row','col'}, use_global_device_ids=true, to_apply=%region_1.2 | all-reduce | flops 16 | bytes 128 | tf_op jit(solution)/shard_map/psum | solution.py:53
  184.8 60.6 %all-gather.1 = f32[256,32,8]{1,2,0:T(8,128)S(1)} all-gather(f32[1,32,8]{1,2,0:T(8,128)S(1)} %convolution_bitcast_fusion.20), channel_id=1, replica_groups=mesh['row'=16,'col'=16] {'row','col'}, dimensions={0}, use_global_device_ids=true | all-gather | bytes 263168 | tf_op jit(solution)/shard_map/all_gather | solution.py:98
  247.4 23.1 %psum.72 = f32[8]{0:T(128)S(1)} all-reduce(f32[8]{0:T(128)S(1)} %get-tuple-element.31), channel_id=1, replica_groups=mesh['row'=16,'col'=16] {'col'}, use_global_device_ids=true, to_apply=%region_6.9 | all-reduce | flops 8 | bytes 64 | tf_op jit(solution)/shard_map/psum | solution.py:116
  270.5 31.0 %psum.73 = f32[8]{0:T(128)S(1)} all-reduce(f32[8]{0:T(128)S(1)} %psum.72), channel_id=1, replica_groups=mesh['row'=16,'col'=16] {'row'}, use_global_device_ids=true, to_apply=%region_7.10 | all-reduce | flops 8 | bytes 64 | tf_op jit(solution)/shard_map/psum | solution.py:116
  305.9 10.6 %collective-permute-start.6 = (f32[8,1,128]{2,0,1:T(8,128)S(1)}, f32[8,1,128]{2,0,1:T(8,128)S(1)}, u32[]{:S(2)}, u32[]{:S(2)}) collective-permute-start(f32[8,1,128]{2,0,1:T(8,128)S(1)} %copy.124), channel_id=1, source_target_pairs={{0,1},{1,2},{2,3},{3,4},{4,5},{5,6},{6,7},{7,8},{8,9},{9,10},{10,1... | collective-permute-start | bytes 12296 | tf_op jit(solution)/shard_map/ppermute | solution.py:18
  316.5 3.6 collective-permute-start.7
  320.9 3.8 convolution_bitcast_fusion.15
  325.6 4.0 convolution_bitcast_fusion.14
  338.3 3.9 scatter_custom_fusion.1
  342.6 75.9 %all-reduce.1 = (f32[8]{0:T(128)S(1)}, f32[8]{0:T(128)S(1)}) all-reduce(f32[8]{0:T(128)S(1)} %get-tuple-element.8, f32[8]{0:T(128)S(1)} %get-tuple-element.7), channel_id=1, replica_groups=mesh['row'=16,'col'=16] {'row','col'}, use_global_device_ids=true, to_apply=%region_9.12 | all-reduce | flops 16 | bytes 128 | tf_op jit(solution)/shard_map/psum | solution.py:53
  418.9 60.8 %all-gather.2 = f32[256,32,8]{1,2,0:T(8,128)S(1)} all-gather(f32[1,32,8]{1,2,0:T(8,128)S(1)} %convolution_bitcast_fusion.19), channel_id=1, replica_groups=mesh['row'=16,'col'=16] {'row','col'}, dimensions={0}, use_global_device_ids=true | all-gather | bytes 263168 | tf_op jit(solution)/shard_map/all_gather | solution.py:98
  481.7 23.1 %psum.76 = f32[8]{0:T(128)S(1)} all-reduce(f32[8]{0:T(128)S(1)} %get-tuple-element.33), channel_id=1, replica_groups=mesh['row'=16,'col'=16] {'col'}, use_global_device_ids=true, to_apply=%region_14.17 | all-reduce | flops 8 | bytes 64 | tf_op jit(solution)/shard_map/psum | solution.py:116
  504.8 30.9 %psum.77 = f32[8]{0:T(128)S(1)} all-reduce(f32[8]{0:T(128)S(1)} %psum.76), channel_id=1, replica_groups=mesh['row'=16,'col'=16] {'row'}, use_global_device_ids=true, to_apply=%region_15.18 | all-reduce | flops 8 | bytes 64 | tf_op jit(solution)/shard_map/psum | solution.py:116
  537.3 10.6 %collective-permute-start.10 = (f32[8,1,128]{2,0,1:T(8,128)S(1)}, f32[8,1,128]{2,0,1:T(8,128)S(1)}, u32[]{:S(2)}, u32[]{:S(2)}) collective-permute-start(f32[8,1,128]{2,0,1:T(8,128)S(1)} %copy.128), channel_id=1, source_target_pairs={{0,1},{1,2},{2,3},{3,4},{4,5},{5,6},{6,7},{7,8},{8,9},{9,10},{10,1... | collective-permute-start | bytes 12296 | tf_op jit(solution)/shard_map/ppermute | solution.py:18
  554.7 3.8 convolution_bitcast_fusion.13
  559.3 4.0 convolution_bitcast_fusion.12
  572.1 3.9 scatter_custom_fusion.2
  576.5 75.5 %all-reduce = (f32[8]{0:T(128)S(1)}, f32[8]{0:T(128)S(1)}) all-reduce(f32[8]{0:T(128)S(1)} %get-tuple-element.6, f32[8]{0:T(128)S(1)} %get-tuple-element.5), channel_id=1, replica_groups=mesh['row'=16,'col'=16] {'row','col'}, use_global_device_ids=true, to_apply=%region_17.20 | all-reduce | flops 16 | bytes 128 | tf_op jit(solution)/shard_map/psum | solution.py:53
  653.0 61.2 %all-gather.3 = f32[256,32,8]{1,2,0:T(8,128)S(1)} all-gather(f32[1,32,8]{1,2,0:T(8,128)S(1)} %convolution_bitcast_fusion.18), channel_id=1, replica_groups=mesh['row'=16,'col'=16] {'row','col'}, dimensions={0}, use_global_device_ids=true | all-gather | bytes 263168 | tf_op jit(solution)/shard_map/all_gather | solution.py:98
  (163 shorter events, 63.7 us)
Async XLA Ops:
  0.6 71.3 %copy-start = (f32[32,8192]{1,0:T(8,128)S(1)}, f32[32,8192]{1,0:T(8,128)}, u32[]{:S(2)}) copy-start(f32[32,8192]{1,0:T(8,128)} %param.19) | copy-start | bytes 3145732
  0.6 72.2 %copy-start.8 = (f32[8,2048]{1,0:T(8,128)S(1)}, f32[8,2048]{1,0:T(8,128)}, u32[]{:S(2)}) copy-start(f32[8,2048]{1,0:T(8,128)} %param.13) | copy-start | bytes 196612
  0.7 72.2 %copy-start.7 = (f32[32,2048]{1,0:T(8,128)S(1)}, f32[32,2048]{1,0:T(8,128)}, u32[]{:S(2)}) copy-start(f32[32,2048]{1,0:T(8,128)} %param.18) | copy-start | bytes 786436
  3.4 80.0 %copy-start.11 = (s32[16,4]{0,1:T(4,128)S(1)}, s32[16,4]{0,1:T(4,128)}, u32[]{:S(2)}) copy-start(s32[16,4]{0,1:T(4,128)} %param.15) | copy-start | bytes 772
  3.4 80.2 %copy-start.10 = (s32[16,4]{0,1:T(4,128)S(1)}, s32[16,4]{0,1:T(4,128)}, u32[]{:S(2)}) copy-start(s32[16,4]{0,1:T(4,128)} %param.17) | copy-start | bytes 772
  3.4 80.4 %copy-start.13 = (s32[1,4]{1,0:T(1,128)S(1)}, s32[1,4]{1,0:T(1,128)}, u32[]{:S(2)}) copy-start(s32[1,4]{1,0:T(1,128)} %param.21) | copy-start | bytes 52
  74.7 27.0 %collective-permute-start = (f32[8,1,128]{2,0,1:T(8,128)S(1)}, f32[8,1,128]{2,0,1:T(8,128)S(1)}, u32[]{:S(2)}, u32[]{:S(2)}) collective-permute-start(f32[8,1,128]{2,0,1:T(8,128)S(1)} %copy.118), channel_id=1, source_target_pairs={{0,16},{16,32},{32,48},{48,64},{64,80},{80,96},{96,112},{112,128},... | collective-permute-start | bytes 12296 | tf_op jit(solution)/shard_map/ppermute | solution.py:18
  77.4 24.3 %collective-permute-start.1 = (f32[8,1,128]{2,0,1:T(8,128)S(1)}, f32[8,1,128]{2,0,1:T(8,128)S(1)}, u32[]{:S(2)}, u32[]{:S(2)}) collective-permute-start(f32[8,1,128]{2,0,1:T(8,128)S(1)} %copy.119), channel_id=1, source_target_pairs={{16,0},{32,16},{48,32},{64,48},{80,64},{96,80},{112,96},{128,112},... | collective-permute-start | bytes 12296 | tf_op jit(solution)/shard_map/ppermute | solution.py:20
  78.8 22.9 %collective-permute-start.2 = (f32[8,1,128]{2,0,1:T(8,128)S(1)}, f32[8,1,128]{2,0,1:T(8,128)S(1)}, u32[]{:S(2)}, u32[]{:S(2)}) collective-permute-start(f32[8,1,128]{2,0,1:T(8,128)S(1)} %copy.120), channel_id=1, source_target_pairs={{0,1},{1,2},{2,3},{3,4},{4,5},{5,6},{6,7},{7,8},{8,9},{9,10},{10,1... | collective-permute-start | bytes 12296 | tf_op jit(solution)/shard_map/ppermute | solution.py:18
  80.8 20.9 %collective-permute-start.3 = (f32[8,1,128]{2,0,1:T(8,128)S(1)}, f32[8,1,128]{2,0,1:T(8,128)S(1)}, u32[]{:S(2)}, u32[]{:S(2)}) collective-permute-start(f32[8,1,128]{2,0,1:T(8,128)S(1)} %copy.121), channel_id=1, source_target_pairs={{1,0},{2,1},{3,2},{4,3},{5,4},{6,5},{7,6},{8,7},{9,8},{10,9},{11,1... | collective-permute-start | bytes 12296 | tf_op jit(solution)/shard_map/ppermute | solution.py:20
  89.2 4.2 copy-start.1
  89.3 8.0 %copy-start.4 = (f32[8192,128]{1,0:T(8,128)S(1)}, f32[8192,128]{1,0:T(8,128)}, u32[]{:S(2)}) copy-start(f32[8192,128]{1,0:T(8,128)} %param.14) | copy-start | bytes 12582916
  93.3 8.0 %copy-start.12 = (s32[4,128]{1,0:T(4,128)S(1)}, s32[4,128]{1,0:T(4,128)}, u32[]{:S(2)}) copy-start(s32[4,128]{1,0:T(4,128)} %param.20) | copy-start | bytes 6148
  303.1 34.8 %collective-permute-start.4 = (f32[8,1,128]{2,0,1:T(8,128)S(1)}, f32[8,1,128]{2,0,1:T(8,128)S(1)}, u32[]{:S(2)}, u32[]{:S(2)}) collective-permute-start(f32[8,1,128]{2,0,1:T(8,128)S(1)} %copy.122), channel_id=1, source_target_pairs={{0,16},{16,32},{32,48},{48,64},{64,80},{80,96},{96,112},{112,128},... | collective-permute-start | bytes 12296 | tf_op jit(solution)/shard_map/ppermute | solution.py:18
  304.5 33.4 %collective-permute-start.5 = (f32[8,1,128]{2,0,1:T(8,128)S(1)}, f32[8,1,128]{2,0,1:T(8,128)S(1)}, u32[]{:S(2)}, u32[]{:S(2)}) collective-permute-start(f32[8,1,128]{2,0,1:T(8,128)S(1)} %copy.123), channel_id=1, source_target_pairs={{16,0},{32,16},{48,32},{64,48},{80,64},{96,80},{112,96},{128,112},... | collective-permute-start | bytes 12296 | tf_op jit(solution)/shard_map/ppermute | solution.py:20
  305.9 32.1 %collective-permute-start.6 = (f32[8,1,128]{2,0,1:T(8,128)S(1)}, f32[8,1,128]{2,0,1:T(8,128)S(1)}, u32[]{:S(2)}, u32[]{:S(2)}) collective-permute-start(f32[8,1,128]{2,0,1:T(8,128)S(1)} %copy.124), channel_id=1, source_target_pairs={{0,1},{1,2},{2,3},{3,4},{4,5},{5,6},{6,7},{7,8},{8,9},{9,10},{10,1... | collective-permute-start | bytes 12296 | tf_op jit(solution)/shard_map/ppermute | solution.py:18
  316.5 21.4 %collective-permute-start.7 = (f32[8,1,128]{2,0,1:T(8,128)S(1)}, f32[8,1,128]{2,0,1:T(8,128)S(1)}, u32[]{:S(2)}, u32[]{:S(2)}) collective-permute-start(f32[8,1,128]{2,0,1:T(8,128)S(1)} %copy.125), channel_id=1, source_target_pairs={{1,0},{2,1},{3,2},{4,3},{5,4},{6,5},{7,6},{8,7},{9,8},{10,9},{11,1... | collective-permute-start | bytes 12296 | tf_op jit(solution)/shard_map/ppermute | solution.py:20
  325.6 8.0 %copy-start.5 = (f32[8192,128]{1,0:T(8,128)S(1)}, f32[8192,128]{1,0:T(8,128)}, u32[]{:S(2)}) copy-start(f32[8192,128]{1,0:T(8,128)} %param.14) | copy-start | bytes 12582916
  537.3 34.3 %collective-permute-start.10 = (f32[8,1,128]{2,0,1:T(8,128)S(1)}, f32[8,1,128]{2,0,1:T(8,128)S(1)}, u32[]{:S(2)}, u32[]{:S(2)}) collective-permute-start(f32[8,1,128]{2,0,1:T(8,128)S(1)} %copy.128), channel_id=1, source_target_pairs={{0,1},{1,2},{2,3},{3,4},{4,5},{5,6},{6,7},{7,8},{8,9},{9,10},{10,1... | collective-permute-start | bytes 12296 | tf_op jit(solution)/shard_map/ppermute | solution.py:18
  548.0 23.6 %collective-permute-start.11 = (f32[8,1,128]{2,0,1:T(8,128)S(1)}, f32[8,1,128]{2,0,1:T(8,128)S(1)}, u32[]{:S(2)}, u32[]{:S(2)}) collective-permute-start(f32[8,1,128]{2,0,1:T(8,128)S(1)} %copy.129), channel_id=1, source_target_pairs={{1,0},{2,1},{3,2},{4,3},{5,4},{6,5},{7,6},{8,7},{9,8},{10,9},{11,1... | collective-permute-start | bytes 12296 | tf_op jit(solution)/shard_map/ppermute | solution.py:20
  551.2 20.4 %collective-permute-start.8 = (f32[8,1,128]{2,0,1:T(8,128)S(1)}, f32[8,1,128]{2,0,1:T(8,128)S(1)}, u32[]{:S(2)}, u32[]{:S(2)}) collective-permute-start(f32[8,1,128]{2,0,1:T(8,128)S(1)} %copy.126), channel_id=1, source_target_pairs={{0,16},{16,32},{32,48},{48,64},{64,80},{80,96},{96,112},{112,128},... | collective-permute-start | bytes 12296 | tf_op jit(solution)/shard_map/ppermute | solution.py:18
  552.6 19.1 %collective-permute-start.9 = (f32[8,1,128]{2,0,1:T(8,128)S(1)}, f32[8,1,128]{2,0,1:T(8,128)S(1)}, u32[]{:S(2)}, u32[]{:S(2)}) collective-permute-start(f32[8,1,128]{2,0,1:T(8,128)S(1)} %copy.127), channel_id=1, source_target_pairs={{16,0},{32,16},{48,32},{64,48},{80,64},{96,80},{112,96},{128,112},... | collective-permute-start | bytes 12296 | tf_op jit(solution)/shard_map/ppermute | solution.py:20
  559.3 8.0 %copy-start.6 = (f32[8192,128]{1,0:T(8,128)S(1)}, f32[8192,128]{1,0:T(8,128)}, u32[]{:S(2)}) copy-start(f32[8192,128]{1,0:T(8,128)} %param.14) | copy-start | bytes 12582916
  652.7 64.0 %copy-start.9 = (f32[8,2048]{1,0:T(8,128)}, f32[8,2048]{1,0:T(8,128)S(1)}, u32[]{:S(2)}) copy-start(f32[8,2048]{1,0:T(8,128)S(1)} %get-tuple-element.29) | copy-start | bytes 196612
  (2 other events, 8.3 us)
